TPU v7x, 32 devices: a whole 2x2x4 slice. The times are simulated.
32 devices in a mesh: gz: 8 (over z, x), gy: 4 (over y, core).
Axes of the slice: x: 2, y: 2, z: 4, core: 2. Of those that a mesh axis runs over, the one named last changes fastest.
Arguments:
- volume: bfloat16 [32, 16, 32, 128], P('gz', 'gy'), may hold values from -6 to 6
- kernel_a: bfloat16 [3, 3, 3, 128, 128], replicated, may hold values from -0.109375 to 0.109375
- bias_a: float32 [128], replicated, may hold values from -3 to 3
- kernel_b: bfloat16 [3, 3, 3, 128, 256], P(None, None, None, None, 'gy'), may hold values from -0.109375 to 0.109375
- bias_b: float32 [256], P('gy'), may hold values from -3 to 3
- kernel_c: bfloat16 [3, 3, 3, 256, 512], P(None, None, None, None, 'gy'), may hold values from -0.078125 to 0.078125
- bias_c: float32 [512], P('gy'), may hold values from -3 to 3
Outputs:
- skip_a: bfloat16 [32, 16, 32, 128], P('gz', 'gy')
- skip_b: bfloat16 [16, 8, 16, 256], P('gz', None, None, 'gy')
- bottom: bfloat16 [8, 4, 8, 512], P('gz', None, None, 'gy')
All inputs are finite; a program needn't handle non-finite values.
Results may differ from a plain program's by a relative error of at most 0.0054.
Values may be sent and summed in bfloat16 or wider, within the bound.
A program may use at most 64 MiB of HBM per device.

v0:
```python
import jax
import jax.numpy as jnp
from jax import lax
from jax.sharding import PartitionSpec as P


def extended(array, sides, width):
    for axis, dim in sides:
        peers, length = (lax.axis_size(axis), array.shape[dim])
        up = [(i, (i + 1) % peers) for i in range(peers - 1)]
        down = [(j, i) for i, j in up]
        last = lax.slice_in_dim(array, length - width, length, axis=dim)
        first = lax.slice_in_dim(array, 0, width, axis=dim)
        before = lax.ppermute(last, axis, up)
        after = lax.ppermute(first, axis, down)
        array = jnp.concatenate([before, array, after], axis=dim)
    return array


def conv_relu(padded, kernel, bias):
    out = lax.conv_general_dilated(
        padded[None],
        kernel,
        (1, 1, 1),
        ((0, 0), (0, 0), (1, 1)),
        dimension_numbers=("NDHWC", "DHWIO", "NDHWC"),
        preferred_element_type=jnp.float32,
    )[0]
    return jnp.maximum(out + bias, 0.0).astype(jnp.bfloat16)


def shrink(field):
    depth, height, width, chans = field.shape
    blocks = field.reshape(depth // 2, 2, height // 2, 2, width // 2, 2, chans)
    return jnp.max(blocks, axis=(1, 3, 5))


def pad_height(field):
    return jnp.pad(field, ((0, 0), (1, 1), (0, 0), (0, 0)))


def on_device(volume, kernel_a, bias_a, kernel_b, bias_b, kernel_c, bias_c):
    padded = extended(volume, (("gz", 0), ("gy", 1)), 1)
    skip_a = conv_relu(padded, kernel_a, bias_a)
    pooled_a = shrink(skip_a)
    gathered = lax.all_gather(pooled_a, "gy", axis=1, tiled=True)
    ready_b = extended(gathered, (("gz", 0),), 1)
    skip_b = conv_relu(pad_height(ready_b), kernel_b, bias_b)
    pooled_b = shrink(skip_b)
    widened = lax.all_gather(pooled_b, "gy", axis=3, tiled=True)
    ready_c = extended(widened, (("gz", 0),), 1)
    bottom = conv_relu(pad_height(ready_c), kernel_c, bias_c)
    return (skip_a, skip_b, bottom)


def solution(mesh):
    return jax.shard_map(
        on_device,
        mesh=mesh,
        in_specs=(
            P("gz", "gy", None, None),
            P(),
            P(),
            P(None, None, None, None, "gy"),
            P("gy"),
            P(None, None, None, None, "gy"),
            P("gy"),
        ),
        out_specs=(P("gz", "gy", None, None), P("gz", None, None, "gy"), P("gz", None, None, "gy")),
        check_vma=False,
    )
```

profile of v0, /device:TPU:24, one launch (start us, length us, event | category | flops | bytes accessed | tf_op | source)
XLA Modules:
  0.0 54.5 jit_solution(7939145247504538104)
XLA Ops:
  0.6 0.0 copy-start
  0.6 0.9 %fusion.45 = (bf16[1,4,32,128]{3,2,1,0:T(8,128)(2,1)S(1)}, bf16[1,4,32,128]{3,2,1,0:T(8,128)(2,1)S(1)}) fusion(bf16[4,4,32,128]{3,2,1,0:T(8,128)(2,1)} %param.7), kind=kLoop, calls=%fused_computation.61 | loop fusion | bytes 131072 | tf_op jit(solution)/shard_map/slice | solution.py:13
  1.6 3.4 %collective-permute-start = (bf16[1,4,32,128]{3,2,1,0:T(8,128)(2,1)S(1)}, bf16[1,4,32,128]{3,2,1,0:T(8,128)(2,1)S(1)}, u32[]{:S(2)}, u32[]{:S(2)}) collective-permute-start(bf16[1,4,32,128]{3,2,1,0:T(8,128)(2,1)S(1)} %get-tuple-element.15), channel_id=1, source_target_pairs={{0,4},{4,8},{8,12},{12,16},{16,20},{20,24},{24,28},{1,5},{5,9},{9,... | collective-permute-start | bytes 98312 | tf_op jit(solution)/shard_map/ppermute | solution.py:14
  5.0 3.3 %collective-permute-start.1 = (bf16[1,4,32,128]{3,2,1,0:T(8,128)(2,1)S(1)}, bf16[1,4,32,128]{3,2,1,0:T(8,128)(2,1)S(1)}, u32[]{:S(2)}, u32[]{:S(2)}) collective-permute-start(bf16[1,4,32,128]{3,2,1,0:T(8,128)(2,1)S(1)} %get-tuple-element.14), channel_id=1, source_target_pairs={{4,0},{8,4},{12,8},{16,12},{20,16},{24,20},{28,24},{5,1},{9,5},{13... | collective-permute-start | bytes 98312 | tf_op jit(solution)/shard_map/ppermute | solution.py:15
  8.3 0.0 collective-permute-done
  8.3 0.9 %constant_dynamic-update-slice_fusion.1 = bf16[6,4,32,128]{3,2,1,0:T(8,128)(2,1)S(1)} fusion(bf16[6,4,32,128]{3,2,1,0:T(8,128)(2,1)S(1)} %constant_dynamic-update-slice_fusion.2, bf16[4,4,32,128]{3,2,1,0:T(8,128)(2,1)} %param.7), kind=kLoop, calls=%fused_computation.52 | loop fusion | bytes 262144
  9.3 1.5 %collective-permute-done.1 = bf16[1,4,32,128]{3,2,1,0:T(8,128)(2,1)S(1)} collective-permute-done((bf16[1,4,32,128]{3,2,1,0:T(8,128)(2,1)S(1)}, bf16[1,4,32,128]{3,2,1,0:T(8,128)(2,1)S(1)}, u32[]{:S(2)}, u32[]{:S(2)}) %collective-permute-start.1) | collective-permute-done | bytes 32800 | tf_op jit(solution)/shard_map/ppermute | solution.py:15
  10.8 0.0 copy-start.4
  10.8 0.0 copy-start.6
  10.8 1.4 %collective-permute-start.2 = (bf16[6,1,32,128]{3,2,1,0:T(8,128)(2,1)S(1)}, bf16[6,1,32,128]{3,2,1,0:T(8,128)(2,1)S(1)}, u32[]{:S(2)}, u32[]{:S(2)}) collective-permute-start(bf16[6,1,32,128]{3,2,1,0:T(8,128)(2,1)S(1)} %get-tuple-element.12), channel_id=1, source_target_pairs={{0,1},{1,2},{2,3},{4,5},{5,6},{6,7},{8,9},{9,10},{10,11},{12,13},{... | collective-permute-start | bytes 147464 | tf_op jit(solution)/shard_map/ppermute | solution.py:14
  12.2 1.3 %collective-permute-start.3 = (bf16[6,1,32,128]{3,2,1,0:T(8,128)(2,1)S(1)}, bf16[6,1,32,128]{3,2,1,0:T(8,128)(2,1)S(1)}, u32[]{:S(2)}, u32[]{:S(2)}) collective-permute-start(bf16[6,1,32,128]{3,2,1,0:T(8,128)(2,1)S(1)} %get-tuple-element.13), channel_id=1, source_target_pairs={{1,0},{2,1},{3,2},{5,4},{6,5},{7,6},{9,8},{10,9},{11,10},{13,12},{... | collective-permute-start | bytes 147464 | tf_op jit(solution)/shard_map/ppermute | solution.py:15
  13.5 0.0 collective-permute-done.2
  13.5 3.6 %collective-permute-done.3 = bf16[6,1,32,128]{3,2,1,0:T(8,128)(2,1)S(1)} collective-permute-done((bf16[6,1,32,128]{3,2,1,0:T(8,128)(2,1)S(1)}, bf16[6,1,32,128]{3,2,1,0:T(8,128)(2,1)S(1)}, u32[]{:S(2)}, u32[]{:S(2)}) %collective-permute-start.3) | collective-permute-done | bytes 49184 | tf_op jit(solution)/shard_map/ppermute | solution.py:15
  17.2 0.1 copy.50
  17.3 0.1 pad.10.clone
  17.4 0.1 copy.37
  17.5 0.0 copy-done.4
  17.5 0.0 copy-done.6
  17.5 0.0 copy-start.1
  17.5 1.3 %convolution_select_fusion = f32[4,4,8,5,128]{4,2,3,1,0:T(8,128)S(1)} fusion(bf16[3,3,3,128,128]{4,3,2,1,0:T(8,128)(2,1)S(1)} %copy-done.4, bf16[6,6,1,7,2,128]{5,3,4,1,0,2:T(8,128)(2,1)S(1)} %slice.31, bf16[6,6,1,8,5,128]{5,3,4,1,0,2:T(8,128)(2,1)S(1)} %copy.37, pred[8,5]{0,1:T(8,128)(4,1)S(1)} %copy-done.6), kind=kOutput, calls=%fused_computation | convolution fusion | flops 567861248 | bytes 1710120 | tf_op jit(solution)/shard_map/conv_general_dilated | solution.py:21
  18.9 0.1 copy.38
  18.9 0.0 copy-start.2
  19.0 0.0 copy-start.5
  19.0 0.0 copy-start.7
  19.0 0.0 copy-done.1
  19.0 0.2 fusion.31
  19.2 6.7 %all_gather.6 = bf16[2,8,16,128]{3,2,0,1:T(8,128)(2,1)S(1)} all-gather(bf16[2,2,16,128]{3,2,0,1:T(8,128)(2,1)S(1)} %copy.39), channel_id=1, replica_groups=mesh['gz'=8,'gy'=4] {'gy'}, dimensions={1}, use_global_device_ids=true | all-gather | bytes 81920 | tf_op jit(solution)/shard_map/all_gather | solution.py:46
  25.9 1.9 %collective-permute-start.4 = (bf16[1,8,16,128]{3,2,0,1:T(8,128)(2,1)S(1)}, bf16[1,8,16,128]{3,2,0,1:T(8,128)(2,1)S(1)}, u32[]{:S(2)}, u32[]{:S(2)}) collective-permute-start(bf16[1,8,16,128]{3,2,0,1:T(8,128)(2,1)S(1)} %get-tuple-element.16), channel_id=1, source_target_pairs={{0,4},{4,8},{8,12},{12,16},{16,20},{20,24},{24,28},{1,5},{5,9},{9,... | collective-permute-start | bytes 98312 | tf_op jit(solution)/shard_map/ppermute | solution.py:14
  27.9 4.8 %collective-permute-start.5 = (bf16[1,8,16,128]{3,2,0,1:T(8,128)(2,1)S(1)}, bf16[1,8,16,128]{3,2,0,1:T(8,128)(2,1)S(1)}, u32[]{:S(2)}, u32[]{:S(2)}) collective-permute-start(bf16[1,8,16,128]{3,2,0,1:T(8,128)(2,1)S(1)} %get-tuple-element.17), channel_id=1, source_target_pairs={{4,0},{8,4},{12,8},{16,12},{20,16},{24,20},{28,24},{5,1},{9,5},{13... | collective-permute-start | bytes 98312 | tf_op jit(solution)/shard_map/ppermute | solution.py:15
  32.7 0.1 fusion.16
  32.8 0.7 %copy.48 = bf16[4,4,32,128]{3,2,1,0:T(8,128)(2,1)} copy(bf16[4,4,32,128]{3,1,2,0:T(4,128)(2,1)S(1)} %fusion.16) | data formatting | bytes 262144
  33.4 0.0 collective-permute-done.4
  33.4 0.8 %collective-permute-done.5 = bf16[1,8,16,128]{3,2,0,1:T(8,128)(2,1)S(1)} collective-permute-done((bf16[1,8,16,128]{3,2,0,1:T(8,128)(2,1)S(1)}, bf16[1,8,16,128]{3,2,0,1:T(8,128)(2,1)S(1)}, u32[]{:S(2)}, u32[]{:S(2)}) %collective-permute-start.5) | collective-permute-done | bytes 32800 | tf_op jit(solution)/shard_map/ppermute | solution.py:15
  34.3 0.1 copy.51
  34.4 0.1 pad.12.clone
  34.5 0.0 copy-done.2
  34.6 0.0 copy-done.5
  34.6 0.0 copy-done.7
  34.6 0.8 %maximum_convert_fusion.1 = (bf16[2,8,8,3,64]{4,2,3,1,0:T(8,128)(2,1)S(1)}, f32[2,8,8,3,64]{4,2,3,1,0:T(8,128)S(1)}) fusion(f32[64]{0:T(128)S(1)} %copy-done.2, bf16[3,3,3,128,64]{3,4,2,1,0:T(8,128)(2,1)S(1)} %copy-done.5, bf16[4,10,1,7,2,128]{5,3,4,1,0,2:T(8,128)(2,1)S(1)} %slice.35, bf16[4,10,1,8,3,128]{5,3,4,1,0,2:T(8,128)(2,1)S(1)} %copy.42, ...), kind=kOutput, calls=%fused_computation.28 | convolution fusion | flops 171196416 | bytes 979224 | tf_op jit(solution)/shard_map/conv_general_dilated | solution.py:21
  35.5 0.1 reduce_max.30
  35.5 0.1 copy.45
  35.7 5.8 %all-gather = bf16[4,8,256]{1,0,2:T(4,128)(2,1)S(1)} all-gather(bf16[4,8,64]{1,0,2:T(4,128)(2,1)S(1)} %copy.45), channel_id=2, replica_groups=mesh['gz'=8,'gy'=4] {'gy'}, dimensions={2}, use_global_device_ids=true | all-gather | bytes 20480 | tf_op jit(solution)/shard_map/all_gather | solution.py:50
  41.5 0.1 copy.46
  41.6 5.1 %collective-permute-start.7 = (bf16[1,4,8,256]{3,2,1,0:T(8,128)(2,1)S(1)}, bf16[1,4,8,256]{3,2,1,0:T(8,128)(2,1)S(1)}, u32[]{:S(2)}, u32[]{:S(2)}) collective-permute-start(bf16[1,4,8,256]{3,2,1,0:T(8,128)(2,1)S(1)} %bitcast.48), channel_id=1, source_target_pairs={{4,0},{8,4},{12,8},{16,12},{20,16},{24,20},{28,24},{5,1},{9,5},{13... | collective-permute-start | bytes 49160 | tf_op jit(solution)/shard_map/ppermute | solution.py:15
  46.7 1.9 %collective-permute-start.6 = (bf16[1,4,8,256]{3,2,1,0:T(8,128)(2,1)S(1)}, bf16[1,4,8,256]{3,2,1,0:T(8,128)(2,1)S(1)}, u32[]{:S(2)}, u32[]{:S(2)}) collective-permute-start(bf16[1,4,8,256]{3,2,1,0:T(8,128)(2,1)S(1)} %bitcast.49), channel_id=1, source_target_pairs={{0,4},{4,8},{8,12},{12,16},{16,20},{20,24},{24,28},{1,5},{5,9},{9,... | collective-permute-start | bytes 49160 | tf_op jit(solution)/shard_map/ppermute | solution.py:14
  48.7 0.0 copy-start.3
  48.8 0.6 %copy.49 = bf16[2,8,16,64]{3,2,1,0:T(8,128)(2,1)} copy(bf16[2,8,16,64]{3,1,2,0:T(8,128)(2,1)S(1)} %fusion.30) | data formatting | bytes 65536
  49.4 0.0 collective-permute-done.7
  49.4 3.9 %collective-permute-done.6 = bf16[1,4,8,256]{3,2,1,0:T(8,128)(2,1)S(1)} collective-permute-done((bf16[1,4,8,256]{3,2,1,0:T(8,128)(2,1)S(1)}, bf16[1,4,8,256]{3,2,1,0:T(8,128)(2,1)S(1)}, u32[]{:S(2)}, u32[]{:S(2)}) %collective-permute-start.6) | collective-permute-done | bytes 16416 | tf_op jit(solution)/shard_map/ppermute | solution.py:14
  53.3 0.0 copy-done
  53.3 0.6 %fusion.25 = f32[1,1,4,8,128]{4,0,3,2,1:T(1,128)S(1)} fusion(bf16[3,3,3,256,128]{4,3,2,1,0:T(8,128)(2,1)S(1)} %copy-done, bf16[1,3,6,8,256]{4,3,2,1,0:T(8,128)(2,1)S(1)} %fusion.37), kind=kOutput, calls=%fused_computation.35 | convolution fusion | flops 51904512 | bytes 1859584 | tf_op jit(solution)/shard_map/conv_general_dilated | solution.py:21
  53.9 0.0 copy-done.3
  53.9 0.6 %maximum_convert_fusion.2 = bf16[1,4,8,128]{3,2,1,0:T(8,128)(2,1)} fusion(f32[1,4,8,128]{3,2,1,0:T(8,128)S(1)} %bitcast.51, f32[128]{0:T(128)S(1)} %copy-done.3), kind=kLoop, calls=%fused_computation.50 | loop fusion | flops 12288 | bytes 25088 | tf_op jit(solution)/shard_map/convert_element_type | solution.py:29
  (16 shorter events, 0.3 us)
Async XLA Ops:
  0.6 52.6 %copy-start = (bf16[3,3,3,256,128]{4,3,2,1,0:T(8,128)(2,1)S(1)}, bf16[3,3,3,256,128]{4,3,2,1,0:T(8,128)(2,1)}, u32[]{:S(2)}) copy-start(bf16[3,3,3,256,128]{4,3,2,1,0:T(8,128)(2,1)} %param.12) | copy-start | bytes 5308420
  1.6 6.7 %collective-permute-start = (bf16[1,4,32,128]{3,2,1,0:T(8,128)(2,1)S(1)}, bf16[1,4,32,128]{3,2,1,0:T(8,128)(2,1)S(1)}, u32[]{:S(2)}, u32[]{:S(2)}) collective-permute-start(bf16[1,4,32,128]{3,2,1,0:T(8,128)(2,1)S(1)} %get-tuple-element.15), channel_id=1, source_target_pairs={{0,4},{4,8},{8,12},{12,16},{16,20},{20,24},{24,28},{1,5},{5,9},{9,... | collective-permute-start | bytes 98312 | tf_op jit(solution)/shard_map/ppermute | solution.py:14
  5.0 5.8 %collective-permute-start.1 = (bf16[1,4,32,128]{3,2,1,0:T(8,128)(2,1)S(1)}, bf16[1,4,32,128]{3,2,1,0:T(8,128)(2,1)S(1)}, u32[]{:S(2)}, u32[]{:S(2)}) collective-permute-start(bf16[1,4,32,128]{3,2,1,0:T(8,128)(2,1)S(1)} %get-tuple-element.14), channel_id=1, source_target_pairs={{4,0},{8,4},{12,8},{16,12},{20,16},{24,20},{28,24},{5,1},{9,5},{13... | collective-permute-start | bytes 98312 | tf_op jit(solution)/shard_map/ppermute | solution.py:15
  10.8 6.7 %copy-start.4 = (bf16[3,3,3,128,128]{4,3,2,1,0:T(8,128)(2,1)S(1)}, bf16[3,3,3,128,128]{4,3,2,1,0:T(8,128)(2,1)}, u32[]{:S(2)}) copy-start(bf16[3,3,3,128,128]{4,3,2,1,0:T(8,128)(2,1)} %param.8) | copy-start | bytes 2654212
  10.8 6.7 %copy-start.6 = (pred[8,5]{0,1:T(8,128)(4,1)S(1)}, pred[8,5]{0,1:T(8,128)(4,1)}, u32[]{:S(2)}) copy-start(pred[8,5]{0,1:T(8,128)(4,1)} %constant.22) | copy-start | bytes 124
  10.8 2.7 %collective-permute-start.2 = (bf16[6,1,32,128]{3,2,1,0:T(8,128)(2,1)S(1)}, bf16[6,1,32,128]{3,2,1,0:T(8,128)(2,1)S(1)}, u32[]{:S(2)}, u32[]{:S(2)}) collective-permute-start(bf16[6,1,32,128]{3,2,1,0:T(8,128)(2,1)S(1)} %get-tuple-element.12), channel_id=1, source_target_pairs={{0,1},{1,2},{2,3},{4,5},{5,6},{6,7},{8,9},{9,10},{10,11},{12,13},{... | collective-permute-start | bytes 147464 | tf_op jit(solution)/shard_map/ppermute | solution.py:14
  12.2 4.9 %collective-permute-start.3 = (bf16[6,1,32,128]{3,2,1,0:T(8,128)(2,1)S(1)}, bf16[6,1,32,128]{3,2,1,0:T(8,128)(2,1)S(1)}, u32[]{:S(2)}, u32[]{:S(2)}) collective-permute-start(bf16[6,1,32,128]{3,2,1,0:T(8,128)(2,1)S(1)} %get-tuple-element.13), channel_id=1, source_target_pairs={{1,0},{2,1},{3,2},{5,4},{6,5},{7,6},{9,8},{10,9},{11,10},{13,12},{... | collective-permute-start | bytes 147464 | tf_op jit(solution)/shard_map/ppermute | solution.py:15
  17.5 1.5 %copy-start.1 = (f32[128]{0:T(128)S(1)}, f32[128]{0:T(128)}, u32[]{:S(2)}) copy-start(f32[128]{0:T(128)} %param.9) | copy-start | bytes 1540
  18.9 15.6 %copy-start.2 = (f32[64]{0:T(128)S(1)}, f32[64]{0:T(128)}, u32[]{:S(2)}) copy-start(f32[64]{0:T(128)} %param.11) | copy-start | bytes 772
  19.0 15.6 %copy-start.5 = (bf16[3,3,3,128,64]{3,4,2,1,0:T(8,128)(2,1)S(1)}, bf16[3,3,3,128,64]{3,4,2,1,0:T(8,128)(2,1)}, u32[]{:S(2)}) copy-start(bf16[3,3,3,128,64]{3,4,2,1,0:T(8,128)(2,1)} %param.10) | copy-start | bytes 1327108
  19.0 15.6 %copy-start.7 = (pred[8,3]{0,1:T(4,128)(4,1)S(1)}, pred[8,3]{0,1:T(4,128)(4,1)}, u32[]{:S(2)}) copy-start(pred[8,3]{0,1:T(4,128)(4,1)} %constant.23) | copy-start | bytes 76
  25.9 7.5 %collective-permute-start.4 = (bf16[1,8,16,128]{3,2,0,1:T(8,128)(2,1)S(1)}, bf16[1,8,16,128]{3,2,0,1:T(8,128)(2,1)S(1)}, u32[]{:S(2)}, u32[]{:S(2)}) collective-permute-start(bf16[1,8,16,128]{3,2,0,1:T(8,128)(2,1)S(1)} %get-tuple-element.16), channel_id=1, source_target_pairs={{0,4},{4,8},{8,12},{12,16},{16,20},{20,24},{24,28},{1,5},{5,9},{9,... | collective-permute-start | bytes 98312 | tf_op jit(solution)/shard_map/ppermute | solution.py:14
  27.9 6.4 %collective-permute-start.5 = (bf16[1,8,16,128]{3,2,0,1:T(8,128)(2,1)S(1)}, bf16[1,8,16,128]{3,2,0,1:T(8,128)(2,1)S(1)}, u32[]{:S(2)}, u32[]{:S(2)}) collective-permute-start(bf16[1,8,16,128]{3,2,0,1:T(8,128)(2,1)S(1)} %get-tuple-element.17), channel_id=1, source_target_pairs={{4,0},{8,4},{12,8},{16,12},{20,16},{24,20},{28,24},{5,1},{9,5},{13... | collective-permute-start | bytes 98312 | tf_op jit(solution)/shard_map/ppermute | solution.py:15
  41.6 7.8 %collective-permute-start.7 = (bf16[1,4,8,256]{3,2,1,0:T(8,128)(2,1)S(1)}, bf16[1,4,8,256]{3,2,1,0:T(8,128)(2,1)S(1)}, u32[]{:S(2)}, u32[]{:S(2)}) collective-permute-start(bf16[1,4,8,256]{3,2,1,0:T(8,128)(2,1)S(1)} %bitcast.48), channel_id=1, source_target_pairs={{4,0},{8,4},{12,8},{16,12},{20,16},{24,20},{28,24},{5,1},{9,5},{13... | collective-permute-start | bytes 49160 | tf_op jit(solution)/shard_map/ppermute | solution.py:15
  46.7 6.5 %collective-permute-start.6 = (bf16[1,4,8,256]{3,2,1,0:T(8,128)(2,1)S(1)}, bf16[1,4,8,256]{3,2,1,0:T(8,128)(2,1)S(1)}, u32[]{:S(2)}, u32[]{:S(2)}) collective-permute-start(bf16[1,4,8,256]{3,2,1,0:T(8,128)(2,1)S(1)} %bitcast.49), channel_id=1, source_target_pairs={{0,4},{4,8},{8,12},{12,16},{16,20},{20,24},{24,28},{1,5},{5,9},{9,... | collective-permute-start | bytes 49160 | tf_op jit(solution)/shard_map/ppermute | solution.py:14
  48.7 5.2 %copy-start.3 = (f32[128]{0:T(128)S(1)}, f32[128]{0:T(128)}, u32[]{:S(2)}) copy-start(f32[128]{0:T(128)} %param.13) | copy-start | bytes 1540
where the time goes:
time: 54.8 us; the launch traced here: 54.5 us
  starting transfers between devices  23.2 us (42%)
  blocking collectives  12.5 us (23%)
  waiting for transfers between devices  9.79 us (18%)
  local copies, waits for them, and re-layouts  4.2 us (8%)
  matrix products  2.75 us (5%)
  other arithmetic  1.04 us (2%)
  between operations  1.02 us (2%)
    ppermute x4, starting transfers between devices, extended(): after = lax.ppermute(first, axis, down)  14.6 us
    ppermute x4, starting transfers between devices, extended(): before = lax.ppermute(last, axis, up)  8.64 us
    all_gather x1, blocking collectives, on_device(): gathered = lax.all_gather(pooled_a, 'gy', axis=1, tiled=True)  6.7 us
    ppermute x4, waiting for transfers between devices, extended(): after = lax.ppermute(first, axis, down)  5.9 us
    all_gather x1, blocking collectives, on_device(): widened = lax.all_gather(pooled_b, 'gy', axis=3, tiled=True)  5.78 us
    ppermute x4, waiting for transfers between devices, extended(): before = lax.ppermute(last, axis, up)  3.88 us
    conv_general_dilated x3, matrix products, conv_relu(): lax.conv_general_dilated(padded[None], kernel, (1, 1, 1), ((0, 0), (0, 0)...  2.75 us
    unnamed x22, local copies, waits for them, and re-layouts  2.49 us
  transfers between devices with their start and end apart: 8, of which 4 were waited for; matrix products, arithmetic and copies ran while one was open for 4% of the time, Pallas kernels for 0%

commit v1 on v0

--- a/solution.py
+++ b/solution.py
@@ -2,6 +2,16 @@
 import jax.numpy as jnp
 from jax import lax
 from jax.sharding import PartitionSpec as P
+
+
+def pass_along(x, mesh_axis, dim):
+    devices = lax.axis_size(mesh_axis)
+    current, tiles = (x, [x])
+    for _ in range(devices - 1):
+        current = lax.ppermute(current, mesh_axis, [(i, (i + 1) % devices) for i in range(devices)])
+        tiles.insert(0, current)
+    merged = jnp.concatenate(tiles, axis=dim)
+    return jnp.roll(merged, (lax.axis_index(mesh_axis) + 1) * x.shape[dim], axis=dim)
 
 
 def extended(array, sides, width):
@@ -43,7 +53,7 @@
     padded = extended(volume, (("gz", 0), ("gy", 1)), 1)
     skip_a = conv_relu(padded, kernel_a, bias_a)
     pooled_a = shrink(skip_a)
-    gathered = lax.all_gather(pooled_a, "gy", axis=1, tiled=True)
+    gathered = pass_along(pooled_a, "gy", 1)
     ready_b = extended(gathered, (("gz", 0),), 1)
     skip_b = conv_relu(pad_height(ready_b), kernel_b, bias_b)
     pooled_b = shrink(skip_b)

time: 54.8 us -> 58.6 us (1.069)
  blocking collectives: 12.5 us -> 7.79 us
  starting transfers between devices: 23.2 us -> 27.6 us
  waiting for transfers between devices: 9.79 us -> 13.5 us
    all_gather x1 -> x0, blocking collectives: 6.7 us -> none  [on_device(): gathered = lax.all_gather(pooled_a, 'gy', axis=1, tiled=True)]
    ppermute x0 -> x3, starting transfers between devices: none -> 4.44 us  [pass_along(): lax.ppermute(current, mesh_axis, [(i, (i + 1) % devices) for i in range(d...]
    ppermute x4, waiting for transfers between devices: 5.9 us -> 1.52 us  [extended(): after = lax.ppermute(first, axis, down)]
    ppermute x0 -> x3, waiting for transfers between devices: none -> 4.36 us  [pass_along(): lax.ppermute(current, mesh_axis, [(i, (i + 1) % devices) for i in range(d...]
    ppermute x4, waiting for transfers between devices: 3.88 us -> 7.57 us  [extended(): before = lax.ppermute(last, axis, up)]
    ppermute x4, starting transfers between devices: 14.6 us -> 10.9 us  [extended(): after = lax.ppermute(first, axis, down)]
    ppermute x4, starting transfers between devices: 8.64 us -> 12.3 us  [extended(): before = lax.ppermute(last, axis, up)]
    all_gather x1, blocking collectives: 5.78 us -> 7.79 us  [on_device(): widened = lax.all_gather(pooled_b, 'gy', axis=3, tiled=True)]
  transfers between devices with their start and end apart: 8 -> 11, of which waited for: 4 -> 7; matrix products, arithmetic and copies ran while one was open for 4% -> 4% of each run, Pallas kernels for 0% -> 0%
where the time goes in v1:
time: 58.6 us; the launch traced here: 58.2 us
  starting transfers between devices  27.6 us (47%)
  waiting for transfers between devices  13.5 us (23%)
  blocking collectives  7.79 us (13%)
  local copies, waits for them, and re-layouts  4.42 us (8%)
  matrix products  2.75 us (5%)
  other arithmetic  1.14 us (2%)
  between operations  1.02 us (2%)
    ppermute x4, starting transfers between devices, extended(): before = lax.ppermute(last, axis, up)  12.3 us
    ppermute x4, starting transfers between devices, extended(): after = lax.ppermute(first, axis, down)  10.9 us
    all_gather x1, blocking collectives, on_device(): widened = lax.all_gather(pooled_b, 'gy', axis=3, tiled=True)  7.79 us
    ppermute x4, waiting for transfers between devices, extended(): before = lax.ppermute(last, axis, up)  7.57 us
    ppermute x3, starting transfers between devices, pass_along(): lax.ppermute(current, mesh_axis, [(i, (i + 1) % devices) for i in range(d...  4.44 us
    ppermute x3, waiting for transfers between devices, pass_along(): lax.ppermute(current, mesh_axis, [(i, (i + 1) % devices) for i in range(d...  4.36 us
    conv_general_dilated x3, matrix products, conv_relu(): lax.conv_general_dilated(padded[None], kernel, (1, 1, 1), ((0, 0), (0, 0)...  2.75 us
    unnamed x21, local copies, waits for them, and re-layouts  2.43 us
  transfers between devices with their start and end apart: 11, of which 7 were waited for; matrix products, arithmetic and copies ran while one was open for 4% of the time, Pallas kernels for 0%

profile of v1, /device:TPU:24, one launch (start us, length us, event | category | flops | bytes accessed | tf_op | source)
XLA Modules:
  0.0 58.2 jit_solution(9975243457209307767)
XLA Ops:
  0.6 0.0 copy-start
  0.6 0.9 %fusion.45 = (bf16[1,4,32,128]{3,2,1,0:T(8,128)(2,1)S(1)}, bf16[1,4,32,128]{3,2,1,0:T(8,128)(2,1)S(1)}) fusion(bf16[4,4,32,128]{3,2,1,0:T(8,128)(2,1)} %param.7), kind=kLoop, calls=%fused_computation.64 | loop fusion | bytes 131072 | tf_op jit(solution)/shard_map/slice | solution.py:23
  1.6 3.4 %collective-permute-start = (bf16[1,4,32,128]{3,2,1,0:T(8,128)(2,1)S(1)}, bf16[1,4,32,128]{3,2,1,0:T(8,128)(2,1)S(1)}, u32[]{:S(2)}, u32[]{:S(2)}) collective-permute-start(bf16[1,4,32,128]{3,2,1,0:T(8,128)(2,1)S(1)} %get-tuple-element.17), channel_id=1, source_target_pairs={{0,4},{4,8},{8,12},{12,16},{16,20},{20,24},{24,28},{1,5},{5,9},{9,... | collective-permute-start | bytes 98312 | tf_op jit(solution)/shard_map/ppermute | solution.py:24
  5.0 3.3 %collective-permute-start.1 = (bf16[1,4,32,128]{3,2,1,0:T(8,128)(2,1)S(1)}, bf16[1,4,32,128]{3,2,1,0:T(8,128)(2,1)S(1)}, u32[]{:S(2)}, u32[]{:S(2)}) collective-permute-start(bf16[1,4,32,128]{3,2,1,0:T(8,128)(2,1)S(1)} %get-tuple-element.16), channel_id=1, source_target_pairs={{4,0},{8,4},{12,8},{16,12},{20,16},{24,20},{28,24},{5,1},{9,5},{13... | collective-permute-start | bytes 98312 | tf_op jit(solution)/shard_map/ppermute | solution.py:25
  8.3 0.0 collective-permute-done
  8.3 0.9 %constant_dynamic-update-slice_fusion.1 = bf16[6,4,32,128]{3,2,1,0:T(8,128)(2,1)S(1)} fusion(bf16[6,4,32,128]{3,2,1,0:T(8,128)(2,1)S(1)} %constant_dynamic-update-slice_fusion.2, bf16[4,4,32,128]{3,2,1,0:T(8,128)(2,1)} %param.7), kind=kLoop, calls=%fused_computation.52 | loop fusion | bytes 262144
  9.3 1.5 %collective-permute-done.1 = bf16[1,4,32,128]{3,2,1,0:T(8,128)(2,1)S(1)} collective-permute-done((bf16[1,4,32,128]{3,2,1,0:T(8,128)(2,1)S(1)}, bf16[1,4,32,128]{3,2,1,0:T(8,128)(2,1)S(1)}, u32[]{:S(2)}, u32[]{:S(2)}) %collective-permute-start.1) | collective-permute-done | bytes 32800 | tf_op jit(solution)/shard_map/ppermute | solution.py:25
  10.8 0.0 copy-start.4
  10.8 0.0 copy-start.6
  10.8 1.4 %collective-permute-start.3 = (bf16[6,1,32,128]{3,2,1,0:T(8,128)(2,1)S(1)}, bf16[6,1,32,128]{3,2,1,0:T(8,128)(2,1)S(1)}, u32[]{:S(2)}, u32[]{:S(2)}) collective-permute-start(bf16[6,1,32,128]{3,2,1,0:T(8,128)(2,1)S(1)} %get-tuple-element.13), channel_id=1, source_target_pairs={{1,0},{2,1},{3,2},{5,4},{6,5},{7,6},{9,8},{10,9},{11,10},{13,12},{... | collective-permute-start | bytes 147464 | tf_op jit(solution)/shard_map/ppermute | solution.py:25
  12.2 3.0 %collective-permute-start.2 = (bf16[6,1,32,128]{3,2,1,0:T(8,128)(2,1)S(1)}, bf16[6,1,32,128]{3,2,1,0:T(8,128)(2,1)S(1)}, u32[]{:S(2)}, u32[]{:S(2)}) collective-permute-start(bf16[6,1,32,128]{3,2,1,0:T(8,128)(2,1)S(1)} %get-tuple-element.12), channel_id=1, source_target_pairs={{0,1},{1,2},{2,3},{4,5},{5,6},{6,7},{8,9},{9,10},{10,11},{12,13},{... | collective-permute-start | bytes 147464 | tf_op jit(solution)/shard_map/ppermute | solution.py:24
  15.3 0.0 collective-permute-done.3
  15.3 0.9 %collective-permute-done.2 = bf16[6,1,32,128]{3,2,1,0:T(8,128)(2,1)S(1)} collective-permute-done((bf16[6,1,32,128]{3,2,1,0:T(8,128)(2,1)S(1)}, bf16[6,1,32,128]{3,2,1,0:T(8,128)(2,1)S(1)}, u32[]{:S(2)}, u32[]{:S(2)}) %collective-permute-start.2) | collective-permute-done | bytes 49184 | tf_op jit(solution)/shard_map/ppermute | solution.py:24
  16.2 0.1 copy.50
  16.3 0.1 pad.10.clone
  16.4 0.1 copy.36
  16.5 0.0 copy-done.4
  16.5 0.0 copy-done.6
  16.5 0.0 copy-start.1
  16.5 1.3 %convolution_select_fusion = f32[4,4,8,5,128]{4,2,3,1,0:T(8,128)S(1)} fusion(bf16[3,3,3,128,128]{4,3,2,1,0:T(8,128)(2,1)S(1)} %copy-done.4, bf16[6,6,1,7,2,128]{5,3,4,1,0,2:T(8,128)(2,1)S(1)} %slice.31, bf16[6,6,1,8,5,128]{5,3,4,1,0,2:T(8,128)(2,1)S(1)} %copy.36, pred[8,5]{0,1:T(8,128)(4,1)S(1)} %copy-done.6), kind=kOutput, calls=%fused_computation | convolution fusion | flops 567861248 | bytes 1710120 | tf_op jit(solution)/shard_map/conv_general_dilated | solution.py:31
  17.9 0.1 copy.37
  18.0 0.0 copy-start.2
  18.0 0.0 copy-start.5
  18.0 0.0 copy-start.7
  18.0 0.0 copy-done.1
  18.0 0.2 fusion.31
  18.2 1.5 %collective-permute-start.4 = (bf16[2,2,16,128]{3,1,2,0:T(2,128)(2,1)S(1)}, bf16[2,2,16,128]{3,1,2,0:T(2,128)(2,1)S(1)}, u32[]{:S(2)}, u32[]{:S(2)}) collective-permute-start(bf16[2,2,16,128]{3,1,2,0:T(2,128)(2,1)S(1)} %fusion.31), channel_id=1, source_target_pairs={{0,1},{1,2},{2,3},{3,0},{4,5},{5,6},{6,7},{7,4},{8,9},{9,10},{10,1... | collective-permute-start | bytes 49160 | tf_op jit(solution)/shard_map/ppermute | solution.py:11
  19.7 1.7 %collective-permute-done.4 = bf16[2,2,16,128]{3,1,2,0:T(2,128)(2,1)S(1)} collective-permute-done((bf16[2,2,16,128]{3,1,2,0:T(2,128)(2,1)S(1)}, bf16[2,2,16,128]{3,1,2,0:T(2,128)(2,1)S(1)}, u32[]{:S(2)}, u32[]{:S(2)}) %collective-permute-start.4) | collective-permute-done | bytes 16416 | tf_op jit(solution)/shard_map/ppermute | solution.py:11
  21.5 1.5 %collective-permute-start.5 = (bf16[2,2,16,128]{3,1,2,0:T(2,128)(2,1)S(1)}, bf16[2,2,16,128]{3,1,2,0:T(2,128)(2,1)S(1)}, u32[]{:S(2)}, u32[]{:S(2)}) collective-permute-start(bf16[2,2,16,128]{3,1,2,0:T(2,128)(2,1)S(1)} %collective-permute-done.4), channel_id=1, source_target_pairs={{0,1},{1,2},{2,3},{3,0},{4,5},{5,6},{6,7},{7,4},{8,9},{9,10},{10,1... | collective-permute-start | bytes 49160 | tf_op jit(solution)/shard_map/ppermute | solution.py:11
  22.9 1.7 %collective-permute-done.5 = bf16[2,2,16,128]{3,1,2,0:T(2,128)(2,1)S(1)} collective-permute-done((bf16[2,2,16,128]{3,1,2,0:T(2,128)(2,1)S(1)}, bf16[2,2,16,128]{3,1,2,0:T(2,128)(2,1)S(1)}, u32[]{:S(2)}, u32[]{:S(2)}) %collective-permute-start.5) | collective-permute-done | bytes 16416 | tf_op jit(solution)/shard_map/ppermute | solution.py:11
  24.6 1.5 %collective-permute-start.6 = (bf16[2,2,16,128]{3,1,2,0:T(2,128)(2,1)S(1)}, bf16[2,2,16,128]{3,1,2,0:T(2,128)(2,1)S(1)}, u32[]{:S(2)}, u32[]{:S(2)}) collective-permute-start(bf16[2,2,16,128]{3,1,2,0:T(2,128)(2,1)S(1)} %collective-permute-done.5), channel_id=1, source_target_pairs={{0,1},{1,2},{2,3},{3,0},{4,5},{5,6},{6,7},{7,4},{8,9},{9,10},{10,1... | collective-permute-start | bytes 49160 | tf_op jit(solution)/shard_map/ppermute | solution.py:11
  26.1 0.1 fusion.22
  26.2 0.7 %copy.46 = bf16[4,4,32,128]{3,2,1,0:T(8,128)(2,1)} copy(bf16[4,4,32,128]{3,1,2,0:T(4,128)(2,1)S(1)} %fusion.22) | data formatting | bytes 262144
  26.8 0.9 %collective-permute-done.6 = bf16[2,2,16,128]{3,1,2,0:T(2,128)(2,1)S(1)} collective-permute-done((bf16[2,2,16,128]{3,1,2,0:T(2,128)(2,1)S(1)}, bf16[2,2,16,128]{3,1,2,0:T(2,128)(2,1)S(1)}, u32[]{:S(2)}, u32[]{:S(2)}) %collective-permute-start.6) | collective-permute-done | bytes 16416 | tf_op jit(solution)/shard_map/ppermute | solution.py:11
  27.8 0.2 concatenate.20
  28.1 4.2 %collective-permute-start.8 = (bf16[1,8,16,128]{3,1,2,0:T(8,128)(2,1)S(1)}, bf16[1,8,16,128]{3,1,2,0:T(8,128)(2,1)S(1)}, u32[]{:S(2)}, u32[]{:S(2)}) collective-permute-start(bf16[1,8,16,128]{3,1,2,0:T(8,128)(2,1)S(1)} %get-tuple-element.15), channel_id=1, source_target_pairs={{4,0},{8,4},{12,8},{16,12},{20,16},{24,20},{28,24},{5,1},{9,5},{13... | collective-permute-start | bytes 98312 | tf_op jit(solution)/shard_map/ppermute | solution.py:25
  32.3 1.9 %collective-permute-start.7 = (bf16[1,8,16,128]{3,1,2,0:T(8,128)(2,1)S(1)}, bf16[1,8,16,128]{3,1,2,0:T(8,128)(2,1)S(1)}, u32[]{:S(2)}, u32[]{:S(2)}) collective-permute-start(bf16[1,8,16,128]{3,1,2,0:T(8,128)(2,1)S(1)} %get-tuple-element.14), channel_id=1, source_target_pairs={{0,4},{4,8},{8,12},{12,16},{16,20},{20,24},{24,28},{1,5},{5,9},{9,... | collective-permute-start | bytes 98312 | tf_op jit(solution)/shard_map/ppermute | solution.py:24
  34.3 0.0 collective-permute-done.8
  34.3 4.8 %collective-permute-done.7 = bf16[1,8,16,128]{3,1,2,0:T(8,128)(2,1)S(1)} collective-permute-done((bf16[1,8,16,128]{3,1,2,0:T(8,128)(2,1)S(1)}, bf16[1,8,16,128]{3,1,2,0:T(8,128)(2,1)S(1)}, u32[]{:S(2)}, u32[]{:S(2)}) %collective-permute-start.7) | collective-permute-done | bytes 32800 | tf_op jit(solution)/shard_map/ppermute | solution.py:24
  39.1 0.1 fusion.20
  39.3 0.1 pad.12
  39.3 0.1 copy.40
  39.5 0.0 copy-done.2
  39.5 0.0 copy-done.5
  39.5 0.0 copy-done.7
  39.5 0.8 %maximum_convert_fusion.1 = (bf16[2,8,8,3,64]{4,2,3,1,0:T(8,128)(2,1)S(1)}, f32[2,8,8,3,64]{4,2,3,1,0:T(8,128)S(1)}) fusion(f32[64]{0:T(128)S(1)} %copy-done.2, bf16[3,3,3,128,64]{3,4,2,1,0:T(8,128)(2,1)S(1)} %copy-done.5, bf16[4,10,1,7,2,128]{5,3,4,1,0,2:T(8,128)(2,1)S(1)} %slice.33, bf16[4,10,1,8,3,128]{5,3,4,1,0,2:T(8,128)(2,1)S(1)} %copy.40, ...), kind=kOutput, calls=%fused_computation.34 | convolution fusion | flops 171196416 | bytes 979224 | tf_op jit(solution)/shard_map/conv_general_dilated | solution.py:31
  40.4 0.1 reduce_max.30
  40.5 0.1 copy.43
  40.6 7.8 %all-gather = bf16[4,8,256]{1,0,2:T(4,128)(2,1)S(1)} all-gather(bf16[4,8,64]{1,0,2:T(4,128)(2,1)S(1)} %copy.43), channel_id=2, replica_groups=mesh['gz'=8,'gy'=4] {'gy'}, dimensions={2}, use_global_device_ids=true | all-gather | bytes 20480 | tf_op jit(solution)/shard_map/all_gather | solution.py:60
  48.4 0.1 copy.44
  48.5 1.9 %collective-permute-start.10 = (bf16[1,4,8,256]{3,2,1,0:T(8,128)(2,1)S(1)}, bf16[1,4,8,256]{3,2,1,0:T(8,128)(2,1)S(1)}, u32[]{:S(2)}, u32[]{:S(2)}) collective-permute-start(bf16[1,4,8,256]{3,2,1,0:T(8,128)(2,1)S(1)} %bitcast.48), channel_id=1, source_target_pairs={{4,0},{8,4},{12,8},{16,12},{20,16},{24,20},{28,24},{5,1},{9,5},{13... | collective-permute-start | bytes 49160 | tf_op jit(solution)/shard_map/ppermute | solution.py:25
  50.5 3.9 %collective-permute-start.9 = (bf16[1,4,8,256]{3,2,1,0:T(8,128)(2,1)S(1)}, bf16[1,4,8,256]{3,2,1,0:T(8,128)(2,1)S(1)}, u32[]{:S(2)}, u32[]{:S(2)}) collective-permute-start(bf16[1,4,8,256]{3,2,1,0:T(8,128)(2,1)S(1)} %bitcast.49), channel_id=1, source_target_pairs={{0,4},{4,8},{8,12},{12,16},{16,20},{20,24},{24,28},{1,5},{5,9},{9,... | collective-permute-start | bytes 49160 | tf_op jit(solution)/shard_map/ppermute | solution.py:24
  54.4 0.0 copy-start.3
  54.5 0.6 %copy.47 = bf16[2,8,16,64]{3,2,1,0:T(8,128)(2,1)} copy(bf16[2,8,16,64]{3,1,2,0:T(8,128)(2,1)S(1)} %fusion.30) | data formatting | bytes 65536
  55.1 0.0 collective-permute-done.10
  55.1 1.9 %collective-permute-done.9 = bf16[1,4,8,256]{3,2,1,0:T(8,128)(2,1)S(1)} collective-permute-done((bf16[1,4,8,256]{3,2,1,0:T(8,128)(2,1)S(1)}, bf16[1,4,8,256]{3,2,1,0:T(8,128)(2,1)S(1)}, u32[]{:S(2)}, u32[]{:S(2)}) %collective-permute-start.9) | collective-permute-done | bytes 16416 | tf_op jit(solution)/shard_map/ppermute | solution.py:24
  57.0 0.0 copy-done
  57.0 0.6 fusion.25
  57.6 0.0 copy-done.3
  57.6 0.6 %maximum_convert_fusion.2 = bf16[1,4,8,128]{3,2,1,0:T(8,128)(2,1)} fusion(f32[1,4,8,128]{3,2,1,0:T(8,128)S(1)} %bitcast.51, f32[128]{0:T(128)S(1)} %copy-done.3), kind=kLoop, calls=%fused_computation.50 | loop fusion | flops 12288 | bytes 25088 | tf_op jit(solution)/shard_map/convert_element_type | solution.py:39
  (14 shorter events, 0.3 us)
Async XLA Ops:
  0.6 56.4 %copy-start = (bf16[3,3,3,256,128]{4,3,2,1,0:T(8,128)(2,1)S(1)}, bf16[3,3,3,256,128]{4,3,2,1,0:T(8,128)(2,1)}, u32[]{:S(2)}) copy-start(bf16[3,3,3,256,128]{4,3,2,1,0:T(8,128)(2,1)} %param.12) | copy-start | bytes 5308420
  1.6 6.7 %collective-permute-start = (bf16[1,4,32,128]{3,2,1,0:T(8,128)(2,1)S(1)}, bf16[1,4,32,128]{3,2,1,0:T(8,128)(2,1)S(1)}, u32[]{:S(2)}, u32[]{:S(2)}) collective-permute-start(bf16[1,4,32,128]{3,2,1,0:T(8,128)(2,1)S(1)} %get-tuple-element.17), channel_id=1, source_target_pairs={{0,4},{4,8},{8,12},{12,16},{16,20},{20,24},{24,28},{1,5},{5,9},{9,... | collective-permute-start | bytes 98312 | tf_op jit(solution)/shard_map/ppermute | solution.py:24
  5.0 5.8 %collective-permute-start.1 = (bf16[1,4,32,128]{3,2,1,0:T(8,128)(2,1)S(1)}, bf16[1,4,32,128]{3,2,1,0:T(8,128)(2,1)S(1)}, u32[]{:S(2)}, u32[]{:S(2)}) collective-permute-start(bf16[1,4,32,128]{3,2,1,0:T(8,128)(2,1)S(1)} %get-tuple-element.16), channel_id=1, source_target_pairs={{4,0},{8,4},{12,8},{16,12},{20,16},{24,20},{28,24},{5,1},{9,5},{13... | collective-permute-start | bytes 98312 | tf_op jit(solution)/shard_map/ppermute | solution.py:25
  10.8 5.7 %copy-start.4 = (bf16[3,3,3,128,128]{4,3,2,1,0:T(8,128)(2,1)S(1)}, bf16[3,3,3,128,128]{4,3,2,1,0:T(8,128)(2,1)}, u32[]{:S(2)}) copy-start(bf16[3,3,3,128,128]{4,3,2,1,0:T(8,128)(2,1)} %param.8) | copy-start | bytes 2654212
  10.8 5.8 %copy-start.6 = (pred[8,5]{0,1:T(8,128)(4,1)S(1)}, pred[8,5]{0,1:T(8,128)(4,1)}, u32[]{:S(2)}) copy-start(pred[8,5]{0,1:T(8,128)(4,1)} %constant.52) | copy-start | bytes 124
  10.8 4.5 %collective-permute-start.3 = (bf16[6,1,32,128]{3,2,1,0:T(8,128)(2,1)S(1)}, bf16[6,1,32,128]{3,2,1,0:T(8,128)(2,1)S(1)}, u32[]{:S(2)}, u32[]{:S(2)}) collective-permute-start(bf16[6,1,32,128]{3,2,1,0:T(8,128)(2,1)S(1)} %get-tuple-element.13), channel_id=1, source_target_pairs={{1,0},{2,1},{3,2},{5,4},{6,5},{7,6},{9,8},{10,9},{11,10},{13,12},{... | collective-permute-start | bytes 147464 | tf_op jit(solution)/shard_map/ppermute | solution.py:25
  12.2 3.9 %collective-permute-start.2 = (bf16[6,1,32,128]{3,2,1,0:T(8,128)(2,1)S(1)}, bf16[6,1,32,128]{3,2,1,0:T(8,128)(2,1)S(1)}, u32[]{:S(2)}, u32[]{:S(2)}) collective-permute-start(bf16[6,1,32,128]{3,2,1,0:T(8,128)(2,1)S(1)} %get-tuple-element.12), channel_id=1, source_target_pairs={{0,1},{1,2},{2,3},{4,5},{5,6},{6,7},{8,9},{9,10},{10,11},{12,13},{... | collective-permute-start | bytes 147464 | tf_op jit(solution)/shard_map/ppermute | solution.py:24
  16.5 1.5 %copy-start.1 = (f32[128]{0:T(128)S(1)}, f32[128]{0:T(128)}, u32[]{:S(2)}) copy-start(f32[128]{0:T(128)} %param.9) | copy-start | bytes 1540
  18.0 21.5 %copy-start.2 = (f32[64]{0:T(128)S(1)}, f32[64]{0:T(128)}, u32[]{:S(2)}) copy-start(f32[64]{0:T(128)} %param.11) | copy-start | bytes 772
  18.0 21.5 %copy-start.5 = (bf16[3,3,3,128,64]{3,4,2,1,0:T(8,128)(2,1)S(1)}, bf16[3,3,3,128,64]{3,4,2,1,0:T(8,128)(2,1)}, u32[]{:S(2)}) copy-start(bf16[3,3,3,128,64]{3,4,2,1,0:T(8,128)(2,1)} %param.10) | copy-start | bytes 1327108
  18.0 21.5 %copy-start.7 = (pred[8,3]{0,1:T(4,128)(4,1)S(1)}, pred[8,3]{0,1:T(4,128)(4,1)}, u32[]{:S(2)}) copy-start(pred[8,3]{0,1:T(4,128)(4,1)} %constant.53) | copy-start | bytes 76
  18.2 3.2 %collective-permute-start.4 = (bf16[2,2,16,128]{3,1,2,0:T(2,128)(2,1)S(1)}, bf16[2,2,16,128]{3,1,2,0:T(2,128)(2,1)S(1)}, u32[]{:S(2)}, u32[]{:S(2)}) collective-permute-start(bf16[2,2,16,128]{3,1,2,0:T(2,128)(2,1)S(1)} %fusion.31), channel_id=1, source_target_pairs={{0,1},{1,2},{2,3},{3,0},{4,5},{5,6},{6,7},{7,4},{8,9},{9,10},{10,1... | collective-permute-start | bytes 49160 | tf_op jit(solution)/shard_map/ppermute | solution.py:11
  21.5 3.2 %collective-permute-start.5 = (bf16[2,2,16,128]{3,1,2,0:T(2,128)(2,1)S(1)}, bf16[2,2,16,128]{3,1,2,0:T(2,128)(2,1)S(1)}, u32[]{:S(2)}, u32[]{:S(2)}) collective-permute-start(bf16[2,2,16,128]{3,1,2,0:T(2,128)(2,1)S(1)} %collective-permute-done.4), channel_id=1, source_target_pairs={{0,1},{1,2},{2,3},{3,0},{4,5},{5,6},{6,7},{7,4},{8,9},{9,10},{10,1... | collective-permute-start | bytes 49160 | tf_op jit(solution)/shard_map/ppermute | solution.py:11
  24.6 3.2 %collective-permute-start.6 = (bf16[2,2,16,128]{3,1,2,0:T(2,128)(2,1)S(1)}, bf16[2,2,16,128]{3,1,2,0:T(2,128)(2,1)S(1)}, u32[]{:S(2)}, u32[]{:S(2)}) collective-permute-start(bf16[2,2,16,128]{3,1,2,0:T(2,128)(2,1)S(1)} %collective-permute-done.5), channel_id=1, source_target_pairs={{0,1},{1,2},{2,3},{3,0},{4,5},{5,6},{6,7},{7,4},{8,9},{9,10},{10,1... | collective-permute-start | bytes 49160 | tf_op jit(solution)/shard_map/ppermute | solution.py:11
  28.1 6.2 %collective-permute-start.8 = (bf16[1,8,16,128]{3,1,2,0:T(8,128)(2,1)S(1)}, bf16[1,8,16,128]{3,1,2,0:T(8,128)(2,1)S(1)}, u32[]{:S(2)}, u32[]{:S(2)}) collective-permute-start(bf16[1,8,16,128]{3,1,2,0:T(8,128)(2,1)S(1)} %get-tuple-element.15), channel_id=1, source_target_pairs={{4,0},{8,4},{12,8},{16,12},{20,16},{24,20},{28,24},{5,1},{9,5},{13... | collective-permute-start | bytes 98312 | tf_op jit(solution)/shard_map/ppermute | solution.py:25
  32.3 6.8 %collective-permute-start.7 = (bf16[1,8,16,128]{3,1,2,0:T(8,128)(2,1)S(1)}, bf16[1,8,16,128]{3,1,2,0:T(8,128)(2,1)S(1)}, u32[]{:S(2)}, u32[]{:S(2)}) collective-permute-start(bf16[1,8,16,128]{3,1,2,0:T(8,128)(2,1)S(1)} %get-tuple-element.14), channel_id=1, source_target_pairs={{0,4},{4,8},{8,12},{12,16},{16,20},{20,24},{24,28},{1,5},{5,9},{9,... | collective-permute-start | bytes 98312 | tf_op jit(solution)/shard_map/ppermute | solution.py:24
  48.5 6.6 %collective-permute-start.10 = (bf16[1,4,8,256]{3,2,1,0:T(8,128)(2,1)S(1)}, bf16[1,4,8,256]{3,2,1,0:T(8,128)(2,1)S(1)}, u32[]{:S(2)}, u32[]{:S(2)}) collective-permute-start(bf16[1,4,8,256]{3,2,1,0:T(8,128)(2,1)S(1)} %bitcast.48), channel_id=1, source_target_pairs={{4,0},{8,4},{12,8},{16,12},{20,16},{24,20},{28,24},{5,1},{9,5},{13... | collective-permute-start | bytes 49160 | tf_op jit(solution)/shard_map/ppermute | solution.py:25
  50.5 6.5 %collective-permute-start.9 = (bf16[1,4,8,256]{3,2,1,0:T(8,128)(2,1)S(1)}, bf16[1,4,8,256]{3,2,1,0:T(8,128)(2,1)S(1)}, u32[]{:S(2)}, u32[]{:S(2)}) collective-permute-start(bf16[1,4,8,256]{3,2,1,0:T(8,128)(2,1)S(1)} %bitcast.49), channel_id=1, source_target_pairs={{0,4},{4,8},{8,12},{12,16},{16,20},{20,24},{24,28},{1,5},{5,9},{9,... | collective-permute-start | bytes 49160 | tf_op jit(solution)/shard_map/ppermute | solution.py:24
  54.4 3.2 %copy-start.3 = (f32[128]{0:T(128)S(1)}, f32[128]{0:T(128)}, u32[]{:S(2)}) copy-start(f32[128]{0:T(128)} %param.13) | copy-start | bytes 1540
